TPU v7x, 256 devices: a whole 4x4x8 slice. The times are simulated.
256 devices in a mesh: dom: 64 (over x, z, y_lo), feat: 4 (over y_hi, core).
Axes of the slice: x: 4, y: 4 (y_hi: 2, y_lo: 2; y = y_hi * 2 + y_lo), z: 8, core: 2. Of those that a mesh axis runs over, the one named last changes fastest.
Arguments:
- embed: bfloat16 [256, 65536], P('feat', 'dom'), may hold values from -6 to 6
- weight: bfloat16 [256, 256], P('feat'), may hold values from -0.375 to 0.375
- cotangent: bfloat16 [256, 65536], P('feat', 'dom'), may hold values from -6 to 6
- edge_masks: int32 [6144, 128, 128], P('dom'), may hold values 0 or 1
- tile_rows: int32 [6144], P('dom'), may hold values from 0 to 7
- tile_owner: int32 [6144, 1], P('dom'), may hold values from 0 to 63; in each aligned block of 96 rows (0 to 95, 96 to 191, ...) at most 2 rows name the same one
- tile_sub: int32 [6144], P('dom'), may hold values from 0 to 7
Outputs:
- output: bfloat16 [256, 65536], P('feat', 'dom')
- embed_grad: float32 [256, 65536], P('feat', 'dom')
- weight_grad: float32 [256, 256], P('feat')
Inputs may be any that keep to these rules, and one draw needn't show every extreme that they name: `tile_owner`: among the 96 tiles of one index of dom no owner is named more than 2 times, a bound that some block reaches.
All inputs are finite; a program needn't handle non-finite values. No bound on the sum of `edge_masks` on one device may be relied on, other than what follows from the above.
Results may differ from a plain program's by a relative error of at most 0.0059.
Values may be sent and summed in bfloat16 or wider, within the bound.
No kernel may reach another device: no remote copies, remote signals or barrier semaphores. Data moves between devices by JAX's collectives and lax.ppermute only.
A program may use at most 64 MiB of HBM per device.

v0:
```python
import math
import jax
import jax.numpy as jnp
from jax import lax
from jax.sharding import PartitionSpec as P


def per_device(embed, weight, cotangent, edge_masks, tile_rows, tile_owner, tile_sub):
    feat_width = embed.shape[0]
    local_nodes = embed.shape[1]
    block_len = edge_masks.shape[1]
    local_blocks = local_nodes // block_len
    dom_count = lax.axis_size("dom")
    nodes_all = local_nodes * dom_count
    block_range = jnp.arange(local_blocks, dtype=jnp.int32)
    col_ids = tile_owner[:, 0] * local_blocks + tile_sub
    own_bf = embed.reshape(feat_width, local_blocks, block_len)
    gathered = lax.all_gather(embed, "dom", axis=1, tiled=True)
    all_blocks = gathered.reshape(feat_width, dom_count * local_blocks, block_len)
    fetched = jnp.take(all_blocks, col_ids, axis=1)
    mask_bf = edge_masks.astype(jnp.bfloat16)
    contrib = jnp.einsum("ftj,tij->fti", fetched, mask_bf, preferred_element_type=jnp.float32)
    row_onehot = (tile_rows[:, None] == block_range[None, :]).astype(jnp.float32)
    neighbour = jnp.einsum("fti,tr->fri", contrib, row_onehot, precision=lax.Precision.HIGHEST)
    row_int = (tile_rows[:, None] == block_range[None, :]).astype(jnp.int32)
    counts = jnp.sum(edge_masks, axis=2)
    degree = jnp.dot(row_int.T, counts)
    inv_root = 1.0 / jnp.sqrt(1.0 + degree.astype(jnp.float32))
    own_blocks = own_bf.astype(jnp.float32)
    aggregate = (
        (own_blocks + neighbour * inv_root[None])
        .astype(jnp.bfloat16)
        .reshape(feat_width, local_nodes)
    )
    pre_act = lax.psum_scatter(
        jnp.einsum("fh,fn->hn", weight, aggregate, preferred_element_type=jnp.float32),
        "feat",
        scatter_dimension=0,
        tiled=True,
    )
    gate_vals = jax.nn.sigmoid(pre_act)
    output = (pre_act * gate_vals).astype(jnp.bfloat16)
    grad_pre = (
        cotangent.astype(jnp.float32) * gate_vals * (1.0 + pre_act * (1.0 - gate_vals))
    ).astype(jnp.bfloat16)
    grad_full = lax.all_gather(grad_pre, "feat", axis=0, tiled=True)
    grad_agg = jnp.einsum("fh,hn->fn", weight, grad_full, preferred_element_type=jnp.float32)
    weight_terms = jnp.einsum("fn,hn->fh", aggregate, grad_full, preferred_element_type=jnp.float32)
    grad_blocks = grad_agg.reshape(feat_width, local_blocks, block_len)
    scaled_grad = (grad_blocks * inv_root[None]).astype(jnp.bfloat16)
    selected = jnp.take(scaled_grad, tile_rows, axis=1)
    partials = jnp.einsum("fti,tij->tfj", selected, mask_bf, preferred_element_type=jnp.float32)
    start = jnp.int32(0)
    inside = (col_ids >= start) & (col_ids < start + lax.axis_size("dom") * local_blocks)
    target = jnp.where(inside, col_ids, lax.axis_size("dom") * local_blocks)
    empty = jnp.zeros((lax.axis_size("dom") * local_blocks, feat_width, block_len), jnp.float32)
    received = lax.psum_scatter(
        empty.at[target].add(partials, mode="drop"), "dom", scatter_dimension=0, tiled=True
    )
    incoming = jnp.transpose(received, (1, 0, 2))
    embed_grad = (grad_blocks + incoming).reshape(feat_width, local_nodes)
    weight_grad = lax.psum(weight_terms, "dom") / math.sqrt(nodes_all)
    return (output, embed_grad, weight_grad)


def solution(mesh):
    in_specs = (
        P("feat", "dom"),
        P("feat", None),
        P("feat", "dom"),
        P("dom", None, None),
        P("dom"),
        P("dom", None),
        P("dom"),
    )
    out_specs = (P("feat", "dom"), P("feat", "dom"), P("feat", None))
    return jax.shard_map(
        per_device, mesh=mesh, in_specs=in_specs, out_specs=out_specs, check_vma=False
    )
```

profile of v0, /device:TPU:16, one launch (start us, length us, event | category | flops | bytes accessed | tf_op | source)
XLA Modules:
  0.0 1295.9 jit_solution(5123875509077076049)
XLA Ops:
  7.2 0.0 copy-start
  7.2 0.0 all-gather.2.cloned.1.call-start
  7.2 0.7 all-gather.2.cloned.1.call-update
  7.9 0.0 reduce-scatter.7.cloned.1.call-start
  8.0 0.9 convert_bitcast_fusion
  8.9 0.0 copy-start.3
  9.0 0.0 copy-start.4
  9.0 0.0 copy-start.2
  9.0 4.5 reduce_sum.9
  13.5 0.0 copy-done.3
  13.5 0.0 copy-done.4
  13.5 0.0 copy-done.2
  13.5 0.1 fusion.24
  13.7 312.7 %all-gather.2.cloned.1.call-done = bf16[64,65536]{1,0:T(8,128)(2,1)} async-done(((bf16[64,1024]{1,0:T(8,128)(2,1)}), bf16[64,65536]{1,0:T(8,128)(2,1)}) %all-gather.2.cloned.1.call-update) | async-done | bytes 8388624 | tf_op jit(solution)/shard_map/all_gather | solution.py:18
  326.3 9.0 copy_bitcast_fusion
  335.4 4.2 gather_fusion
  339.6 5.0 convolution_bitcast_fusion
  344.6 0.0 copy-start.1
  344.6 2.9 fusion.20
  347.5 0.0 copy-done
  347.5 0.3 convolution_bitcast_fusion.1
  347.9 1.3 copy.39
  349.2 0.0 reduce-scatter.7.cloned.1.call-update
  349.2 0.0 all-reduce.2.cloned.1.call-start
  349.3 31.4 %reduce-scatter.7.cloned.1.call-done = f32[64,1024]{1,0:T(8,128)} async-done(((f32[256,1024]{1,0:T(8,128)}), f32[64,1024]{1,0:T(8,128)}) %reduce-scatter.7.cloned.1.call-update) | async-done | bytes 262160 | tf_op jit(solution)/shard_map/reduce_scatter | solution.py:35
  380.7 0.0 copy-done.1
  380.7 1.7 multiply_convert_fusion
  382.4 8.9 all_gather.7
  391.4 0.9 fusion.29
  392.3 0.2 convolution_bitcast_fusion.2
  392.5 0.0 all-reduce.2.cloned.1.call-update
  392.5 0.2 reduce-scatter.5.cloned.1.call-start
  392.8 2.0 gather_fusion.1
  394.7 4.3 fusion.2
  399.0 7.9 broadcast_in_dim.39
  406.9 13.4 %scatter_fusion = f32[512,64,128]{2,1,0:T(8,128)} fusion(f32[512,64,128]{2,1,0:T(8,128)} %broadcast_in_dim.39, s32[96]{0:T(128)S(1)} %compare_select_fusion.1, f32[96,64,128]{2,1,0:T(8,128)S(1)} %fusion.2), kind=kCustom, calls=%fused_computation.2 | custom fusion | flops 786432 | bytes 9437568 | tf_op jit(solution)/shard_map/scatter-add | solution.py:58
  420.3 0.0 reduce-scatter.5.cloned.1.call-update
  420.4 498.3 %all-reduce.2.cloned.1.call-done = f32[64,256]{1,0:T(8,128)} async-done(((f32[64,256]{1,0:T(8,128)}), f32[64,256]{1,0:T(8,128)}) %all-reduce.2.cloned.1.call-update) | async-done | bytes 65552 | tf_op jit(solution)/shard_map/psum | solution.py:62
  918.6 1.5 broadcast_multiply_fusion
  920.1 367.6 %reduce-scatter.5.cloned.1.call-done = f32[8,64,128]{2,1,0:T(8,128)} async-done(((f32[512,64,128]{2,1,0:T(8,128)}), f32[8,64,128]{2,1,0:T(8,128)}) %reduce-scatter.5.cloned.1.call-update) | async-done | bytes 262160 | tf_op jit(solution)/shard_map/reduce_scatter | solution.py:57
  1287.7 1.7 copy_bitcast_fusion.1
  (8 shorter events, 0.1 us)
Async XLA Ops:
  7.2 340.3 %copy-start = (bf16[64,256]{1,0:T(8,128)(2,1)S(1)}, bf16[64,256]{1,0:T(8,128)(2,1)}, u32[]{:S(2)}) copy-start(bf16[64,256]{1,0:T(8,128)(2,1)} %param.8) | copy-start | bytes 98308
  7.2 319.2 %all-gather.2.cloned.1.call-start = ((), (), s32[]{:S(2)}) async-start(), calls=%async_computation.2 | async-start | bytes 8519680 | tf_op jit(solution)/shard_map/all_gather | solution.py:18
  7.9 372.8 %reduce-scatter.7.cloned.1.call-start = ((), (), s32[]{:S(2)}) async-start(), calls=%async_computation.5 | async-start | bytes 1310720 | tf_op jit(solution)/shard_map/reduce_scatter | solution.py:35
  8.9 4.5 copy-start.3
  9.0 4.5 copy-start.4
  9.0 4.6 copy-start.2
  344.6 36.1 %copy-start.1 = (bf16[64,1024]{1,0:T(8,128)(2,1)S(1)}, bf16[64,1024]{1,0:T(8,128)(2,1)}, u32[]{:S(2)}) copy-start(bf16[64,1024]{1,0:T(8,128)(2,1)} %param.9) | copy-start | bytes 393220
  349.2 569.5 %all-reduce.2.cloned.1.call-start = ((), (), s32[]{:S(2)}) async-start(), calls=%async_computation.4 | async-start | bytes 131072 | tf_op jit(solution)/shard_map/psum | solution.py:62
  392.5 895.2 %reduce-scatter.5.cloned.1.call-start = ((), (), s32[]{:S(2)}) async-start(), calls=%async_computation.3 | async-start | bytes 17039360 | tf_op jit(solution)/shard_map/reduce_scatter | solution.py:57
Sparse Core Ops, SparseCore 0:
  9.8 316.4 all-gather.1
  349.3 31.3 reduce-scatter.6
  392.6 525.9 all-reduce.1
  921.1 366.5 reduce-scatter.4
where the time goes:
time: 1300 us
  waiting for transfers between devices  1210 us (93%)
  local copies, waits for them, and re-layouts  24.5 us (2%)
  other arithmetic  23.8 us (2%)
  between operations  13.9 us (1%)
  matrix products  13.8 us (1%)
    psum x1, waiting for transfers between devices, per_device(): weight_grad = lax.psum(weight_terms, 'dom') / math.sqrt(nodes_all)  498 us
    reduce_scatter x1, waiting for transfers between devices, per_device(): lax.psum_scatter(empty.at[target].add(partials, mode='drop'), 'dom', scat...  368 us
    all_gather x1, waiting for transfers between devices, per_device(): gathered = lax.all_gather(embed, 'dom', axis=1, tiled=True)  313 us
    reduce_scatter x1, waiting for transfers between devices, per_device(): lax.psum_scatter(jnp.einsum('fh,fn->hn', weight, aggregate, preferred_ele...  31.4 us
  transfers between devices with their start and end apart: 4, of which 4 were waited for; matrix products, arithmetic and copies ran while one was open for 3% of the time, Pallas kernels for 0%

commit v1 on v0

--- a/solution.py
+++ b/solution.py
@@ -59,7 +59,7 @@
     )
     incoming = jnp.transpose(received, (1, 0, 2))
     embed_grad = (grad_blocks + incoming).reshape(feat_width, local_nodes)
-    weight_grad = lax.psum(weight_terms, "dom") / math.sqrt(nodes_all)
+    weight_grad = jnp.sum(lax.all_gather(weight_terms, "dom"), axis=0) / math.sqrt(nodes_all)
     return (output, embed_grad, weight_grad)
 
 

time: 1300 us -> 1080 us (0.83)
  waiting for transfers between devices: 1210 us -> 991 us
    psum x1 -> x0, waiting for transfers between devices: 498 us -> none  [per_device(): weight_grad = lax.psum(weight_terms, 'dom') / math.sqrt(nodes_all)]
    all_gather x0 -> x1, waiting for transfers between devices: none -> 278 us  [per_device(): lax.all_gather(weight_terms, 'dom')]
where the time goes in v1:
time: 1080 us
  waiting for transfers between devices  991 us (92%)
  other arithmetic  25.4 us (2%)
  local copies, waits for them, and re-layouts  24.5 us (2%)
  between operations  13.9 us (1%)
  matrix products  13.8 us (1%)
    reduce_scatter x1, waiting for transfers between devices, per_device(): lax.psum_scatter(empty.at[target].add(partials, mode='drop'), 'dom', scat...  368 us
    all_gather x1, waiting for transfers between devices, per_device(): gathered = lax.all_gather(embed, 'dom', axis=1, tiled=True)  313 us
    all_gather x1, waiting for transfers between devices, per_device(): lax.all_gather(weight_terms, 'dom')  278 us
    reduce_scatter x1, waiting for transfers between devices, per_device(): lax.psum_scatter(jnp.einsum('fh,fn->hn', weight, aggregate, preferred_ele...  31.5 us
  transfers between devices with their start and end apart: 4, of which 4 were waited for; matrix products, arithmetic and copies ran while one was open for 3% of the time, Pallas kernels for 0%

profile of v1, /device:TPU:16, one launch (start us, length us, event | category | flops | bytes accessed | tf_op | source)
XLA Modules:
  0.0 1077.4 jit_solution(7739961841324449465)
XLA Ops:
  7.2 0.0 copy-start
  7.2 0.0 all-gather.4.cloned.1.call-start
  7.2 0.7 all-gather.4.cloned.1.call-update
  7.9 0.0 reduce-scatter.7.cloned.1.call-start
  8.0 0.9 convert_bitcast_fusion
  8.9 0.0 copy-start.3
  9.0 0.0 copy-start.4
  9.0 0.0 copy-start.2
  9.0 4.5 reduce_sum.18
  13.5 0.0 copy-done.3
  13.5 0.0 copy-done.4
  13.5 0.0 copy-done.2
  13.5 0.1 fusion.24
  13.7 312.7 %all-gather.4.cloned.1.call-done = bf16[64,65536]{1,0:T(8,128)(2,1)} async-done(((bf16[64,1024]{1,0:T(8,128)(2,1)}), bf16[64,65536]{1,0:T(8,128)(2,1)}) %all-gather.4.cloned.1.call-update) | async-done | bytes 8388624 | tf_op jit(solution)/shard_map/all_gather | solution.py:18
  326.3 9.0 copy_bitcast_fusion
  335.4 4.2 gather_fusion
  339.6 5.0 convolution_bitcast_fusion
  344.6 0.0 copy-start.1
  344.6 2.9 fusion.20
  347.5 0.0 copy-done
  347.5 0.3 convolution_bitcast_fusion.1
  347.9 1.3 copy.39
  349.2 0.0 reduce-scatter.7.cloned.1.call-update
  349.2 0.0 all-gather.6.cloned.1.call-start
  349.2 31.5 %reduce-scatter.7.cloned.1.call-done = f32[64,1024]{1,0:T(8,128)} async-done(((f32[256,1024]{1,0:T(8,128)}), f32[64,1024]{1,0:T(8,128)}) %reduce-scatter.7.cloned.1.call-update) | async-done | bytes 262160 | tf_op jit(solution)/shard_map/reduce_scatter | solution.py:35
  380.7 0.0 copy-done.1
  380.7 1.7 multiply_convert_fusion
  382.4 8.9 all_gather.13
  391.4 0.9 fusion.29
  392.3 0.0 all-gather.6.cloned.1.call-update
  392.3 0.2 reduce-scatter.5.cloned.1.call-start
  392.6 0.2 convolution_bitcast_fusion.2
  392.8 2.0 gather_fusion.1
  394.8 4.3 fusion.2
  399.1 7.9 broadcast_in_dim.39
  406.9 13.4 %scatter_fusion = f32[512,64,128]{2,1,0:T(8,128)} fusion(f32[512,64,128]{2,1,0:T(8,128)} %broadcast_in_dim.39, s32[96]{0:T(128)S(1)} %compare_select_fusion.1, f32[96,64,128]{2,1,0:T(8,128)S(1)} %fusion.2), kind=kCustom, calls=%fused_computation.2 | custom fusion | flops 786432 | bytes 9437568 | tf_op jit(solution)/shard_map/scatter-add | solution.py:58
  420.4 0.0 reduce-scatter.5.cloned.1.call-update
  420.4 277.5 %all-gather.6.cloned.1.call-done = f32[4096,256]{1,0:T(8,128)} async-done(((f32[64,256]{1,0:T(8,128)}), f32[4096,256]{1,0:T(8,128)}) %all-gather.6.cloned.1.call-update) | async-done | bytes 4194320 | tf_op jit(solution)/shard_map/all_gather | solution.py:62
  697.9 2.4 reduce_sum.19
  700.4 0.6 broadcast_multiply_fusion
  701.0 368.2 %reduce-scatter.5.cloned.1.call-done = f32[8,64,128]{2,1,0:T(8,128)} async-done(((f32[512,64,128]{2,1,0:T(8,128)}), f32[8,64,128]{2,1,0:T(8,128)}) %reduce-scatter.5.cloned.1.call-update) | async-done | bytes 262160 | tf_op jit(solution)/shard_map/reduce_scatter | solution.py:57
  1069.2 1.7 copy_bitcast_fusion.1
  (8 shorter events, 0.1 us)
Async XLA Ops:
  7.2 340.3 %copy-start = (bf16[64,256]{1,0:T(8,128)(2,1)S(1)}, bf16[64,256]{1,0:T(8,128)(2,1)}, u32[]{:S(2)}) copy-start(bf16[64,256]{1,0:T(8,128)(2,1)} %param.8) | copy-start | bytes 98308
  7.2 319.2 %all-gather.4.cloned.1.call-start = ((), (), s32[]{:S(2)}) async-start(), calls=%async_computation.2 | async-start | bytes 8519680 | tf_op jit(solution)/shard_map/all_gather | solution.py:18
  7.9 372.8 %reduce-scatter.7.cloned.1.call-start = ((), (), s32[]{:S(2)}) async-start(), calls=%async_computation.5 | async-start | bytes 1310720 | tf_op jit(solution)/shard_map/reduce_scatter | solution.py:35
  8.9 4.5 copy-start.3
  9.0 4.5 copy-start.4
  9.0 4.6 copy-start.2
  344.6 36.1 %copy-start.1 = (bf16[64,1024]{1,0:T(8,128)(2,1)S(1)}, bf16[64,1024]{1,0:T(8,128)(2,1)}, u32[]{:S(2)}) copy-start(bf16[64,1024]{1,0:T(8,128)(2,1)} %param.9) | copy-start | bytes 393220
  349.2 348.8 %all-gather.6.cloned.1.call-start = ((), (), s32[]{:S(2)}) async-start(), calls=%async_computation.4 | async-start | bytes 4259840 | tf_op jit(solution)/shard_map/all_gather | solution.py:62
  392.3 676.9 %reduce-scatter.5.cloned.1.call-start = ((), (), s32[]{:S(2)}) async-start(), calls=%async_computation.3 | async-start | bytes 17039360 | tf_op jit(solution)/shard_map/reduce_scatter | solution.py:57
Sparse Core Ops, SparseCore 0:
  9.8 316.4 all-gather.3
  349.3 31.3 reduce-scatter.6
  392.4 305.4 all-gather.5
  700.5 368.6 reduce-scatter.4

commit v2 on v0

--- a/solution.py
+++ b/solution.py
@@ -15,7 +15,9 @@
     block_range = jnp.arange(local_blocks, dtype=jnp.int32)
     col_ids = tile_owner[:, 0] * local_blocks + tile_sub
     own_bf = embed.reshape(feat_width, local_blocks, block_len)
-    gathered = lax.all_gather(embed, "dom", axis=1, tiled=True)
+    gathered = jnp.concatenate(
+        lax.all_to_all(jnp.stack([embed] * lax.axis_size("dom")), "dom", 0, 0), axis=1
+    )
     all_blocks = gathered.reshape(feat_width, dom_count * local_blocks, block_len)
     fetched = jnp.take(all_blocks, col_ids, axis=1)
     mask_bf = edge_masks.astype(jnp.bfloat16)

time: 1300 us -> 1210 us (0.931)
  waiting for transfers between devices: 1210 us -> 1080 us
  local copies, waits for them, and re-layouts: 24.5 us -> 57.3 us
  starting transfers between devices: 0.34 us -> 13.4 us
    all_gather x1 -> x0, waiting for transfers between devices: 313 us -> none  [per_device(): gathered = lax.all_gather(embed, 'dom', axis=1, tiled=True)]
    all_to_all x0 -> x1, waiting for transfers between devices: none -> 183 us  [per_device(): lax.all_to_all(jnp.stack([embed] * lax.axis_size('dom')), 'dom', 0, 0)]
    another operation x0 -> x3, local copies, waits for them, and re-layouts: none -> 30.5 us  [the longest x2 25.3 us: per_device(): gathered.reshape(feat_width, dom_count * local_blocks, block_len)]
    all_to_all x0 -> x1, starting transfers between devices: none -> 13 us  [per_device(): lax.all_to_all(jnp.stack([embed] * lax.axis_size('dom')), 'dom', 0, 0)]
where the time goes in v2:
time: 1210 us
  waiting for transfers between devices  1080 us (89%)
  local copies, waits for them, and re-layouts  57.3 us (5%)
  other arithmetic  22.9 us (2%)
  between operations  13.9 us (1%)
  matrix products  13.8 us (1%)
  starting transfers between devices  13.4 us (1%)
    psum x1, waiting for transfers between devices, per_device(): weight_grad = lax.psum(weight_terms, 'dom') / math.sqrt(nodes_all)  499 us
    reduce_scatter x1, waiting for transfers between devices, per_device(): lax.psum_scatter(empty.at[target].add(partials, mode='drop'), 'dom', scat...  368 us
    all_to_all x1, waiting for transfers between devices, per_device(): lax.all_to_all(jnp.stack([embed] * lax.axis_size('dom')), 'dom', 0, 0)  183 us
    reduce_scatter x1, waiting for transfers between devices, per_device(): lax.psum_scatter(jnp.einsum('fh,fn->hn', weight, aggregate, preferred_ele...  33.1 us
    another operation x2, local copies, waits for them, and re-layouts, per_device(): gathered.reshape(feat_width, dom_count * local_blocks, block_len)  25.3 us
  transfers between devices with their start and end apart: 4, of which 4 were waited for; matrix products, arithmetic and copies ran while one was open for 3% of the time, Pallas kernels for 0%

profile of v2, /device:TPU:16, one launch (start us, length us, event | category | flops | bytes accessed | tf_op | source)
XLA Modules:
  0.0 1212.7 jit_solution(490654940084653423)
XLA Ops:
  7.2 0.0 copy-start
  7.2 5.2 stack.2
  12.4 0.0 copy-start.1
  12.4 13.0 %all-to-all-start = ((bf16[64,64,1024]{2,1,0:T(8,128)(2,1)}), bf16[64,64,1024]{2,1,0:T(8,128)(2,1)}, u32[]{:S(2)}, u32[]{:S(2)}) async-start(bf16[64,64,1024]{2,1,0:T(8,128)(2,1)} %stack.2), calls=%async_computation | async-start | bytes 16777216 | tf_op jit(solution)/shard_map/all_to_all | solution.py:19
  25.4 0.0 reduce-scatter.7.cloned.1.call-start
  25.5 0.0 copy-done.1
  25.6 0.0 copy-start.4
  25.6 0.0 copy-start.5
  25.6 0.0 copy-start.3
  25.6 4.5 reduce_sum.9
  30.1 0.0 copy-done.4
  30.1 0.0 copy-done.5
  30.2 0.0 copy-done.3
  30.2 0.1 fusion.24
  30.3 182.6 %all-to-all-done = bf16[64,64,1024]{2,1,0:T(8,128)(2,1)} async-done(((bf16[64,64,1024]{2,1,0:T(8,128)(2,1)}), bf16[64,64,1024]{2,1,0:T(8,128)(2,1)}, u32[]{:S(2)}, u32[]{:S(2)}) %all-to-all-start) | async-done | bytes 8388640 | tf_op jit(solution)/shard_map/all_to_all | solution.py:19
  212.9 11.3 copy.33
  224.2 13.3 %reshape_reshape.3 = bf16[64,512,128]{2,1,0:T(8,128)(2,1)} reshape(bf16[64,64,1024]{2,1,0:T(8,128)(2,1)} %copy.33) | data formatting | bytes 16777216 | tf_op jit(solution)/shard_map/reshape;reshape | solution.py:21
  237.5 12.0 copy.34
  249.5 4.2 gather_fusion
  253.8 5.0 convolution_bitcast_fusion
  258.8 0.0 copy-start.2
  258.8 2.9 fusion.20
  261.7 0.0 copy-done
  261.7 0.3 convolution_bitcast_fusion.1
  262.0 1.3 copy.42
  263.3 0.0 reduce-scatter.7.cloned.1.call-update
  263.3 0.0 all-reduce.2.cloned.1.call-start
  263.4 33.1 %reduce-scatter.7.cloned.1.call-done = f32[64,1024]{1,0:T(8,128)} async-done(((f32[256,1024]{1,0:T(8,128)}), f32[64,1024]{1,0:T(8,128)}) %reduce-scatter.7.cloned.1.call-update) | async-done | bytes 262160 | tf_op jit(solution)/shard_map/reduce_scatter | solution.py:37
  296.5 0.0 copy-done.2
  296.5 1.7 multiply_convert_fusion
  298.3 8.9 all_gather.3
  307.2 0.9 fusion.29
  308.1 0.2 convolution_bitcast_fusion.2
  308.3 0.0 all-reduce.2.cloned.1.call-update
  308.3 0.3 reduce-scatter.5.cloned.1.call-start
  308.6 2.0 gather_fusion.1
  310.6 4.3 fusion.2
  314.9 7.9 broadcast_in_dim.39
  322.7 13.4 %scatter_fusion = f32[512,64,128]{2,1,0:T(8,128)} fusion(f32[512,64,128]{2,1,0:T(8,128)} %broadcast_in_dim.39, s32[96]{0:T(128)S(1)} %compare_select_fusion.1, f32[96,64,128]{2,1,0:T(8,128)S(1)} %fusion.2), kind=kCustom, calls=%fused_computation.2 | custom fusion | flops 786432 | bytes 9437568 | tf_op jit(solution)/shard_map/scatter-add | solution.py:60
  336.2 0.0 reduce-scatter.5.cloned.1.call-update
  336.2 499.0 %all-reduce.2.cloned.1.call-done = f32[64,256]{1,0:T(8,128)} async-done(((f32[64,256]{1,0:T(8,128)}), f32[64,256]{1,0:T(8,128)}) %all-reduce.2.cloned.1.call-update) | async-done | bytes 65552 | tf_op jit(solution)/shard_map/psum | solution.py:64
  835.2 1.5 broadcast_multiply_fusion
  836.7 367.7 %reduce-scatter.5.cloned.1.call-done = f32[8,64,128]{2,1,0:T(8,128)} async-done(((f32[512,64,128]{2,1,0:T(8,128)}), f32[8,64,128]{2,1,0:T(8,128)}) %reduce-scatter.5.cloned.1.call-update) | async-done | bytes 262160 | tf_op jit(solution)/shard_map/reduce_scatter | solution.py:59
  1204.5 1.7 copy_bitcast_fusion
  (9 shorter events, 0.1 us)
Async XLA Ops:
  7.2 254.5 %copy-start = (bf16[64,256]{1,0:T(8,128)(2,1)S(1)}, bf16[64,256]{1,0:T(8,128)(2,1)}, u32[]{:S(2)}) copy-start(bf16[64,256]{1,0:T(8,128)(2,1)} %param.8) | copy-start | bytes 98308
  12.4 13.1 %copy-start.1 = (bf16[64,1024]{1,0:T(8,128)(2,1)S(1)}, bf16[64,1024]{1,0:T(8,128)(2,1)}, u32[]{:S(2)}) copy-start(bf16[64,1024]{1,0:T(8,128)(2,1)} %param.7) | copy-start | bytes 393220
  12.4 200.5 %all-to-all-start = ((bf16[64,64,1024]{2,1,0:T(8,128)(2,1)}), bf16[64,64,1024]{2,1,0:T(8,128)(2,1)}, u32[]{:S(2)}, u32[]{:S(2)}) async-start(bf16[64,64,1024]{2,1,0:T(8,128)(2,1)} %stack.2), calls=%async_computation | async-start | bytes 16777216 | tf_op jit(solution)/shard_map/all_to_all | solution.py:19
  25.4 271.1 %reduce-scatter.7.cloned.1.call-start = ((), (), s32[]{:S(2)}) async-start(), calls=%async_computation.5 | async-start | bytes 1310720 | tf_op jit(solution)/shard_map/reduce_scatter | solution.py:37
  25.6 4.5 copy-start.4
  25.6 4.5 copy-start.5
  25.6 4.6 copy-start.3
  258.8 37.8 %copy-start.2 = (bf16[64,1024]{1,0:T(8,128)(2,1)S(1)}, bf16[64,1024]{1,0:T(8,128)(2,1)}, u32[]{:S(2)}) copy-start(bf16[64,1024]{1,0:T(8,128)(2,1)} %param.9) | copy-start | bytes 393220
  263.3 571.9 %all-reduce.2.cloned.1.call-start = ((), (), s32[]{:S(2)}) async-start(), calls=%async_computation.4 | async-start | bytes 131072 | tf_op jit(solution)/shard_map/psum | solution.py:64
  308.3 896.1 %reduce-scatter.5.cloned.1.call-start = ((), (), s32[]{:S(2)}) async-start(), calls=%async_computation.3 | async-start | bytes 17039360 | tf_op jit(solution)/shard_map/reduce_scatter | solution.py:59
Sparse Core Ops, SparseCore 0:
  263.5 33.0 reduce-scatter.6
  308.4 526.7 all-reduce.1
  837.8 366.6 reduce-scatter.4
